TPU v7x, 32 devices: a whole 2x2x4 slice. The times are simulated.
32 devices in a mesh: seq: 4 (over z), fsdp: 8 (over y, x, core).
Axes of the slice: x: 2, y: 2, z: 4, core: 2. Of those that a mesh axis runs over, the one named last changes fastest.
Arguments:
- tokens: bfloat16 [8, 512, 768], P('fsdp', 'seq'), may hold values from -6 to 6
- positions: int32 [8, 512], P('fsdp', 'seq'), may hold values from 0 to 5117, as said below
- norm1_gain: bfloat16 [768], P('fsdp'), may hold values from 0.5 to 1.5
- qkv_weight: bfloat16 [768, 2304], P('fsdp'), may hold values from -0.57735027 to 0.57735027, as said below
- out_weight: bfloat16 [768, 768], P('fsdp'), may hold values from -6 to 6
- norm2_gain: bfloat16 [768], P('fsdp'), may hold values from 0.5 to 1.5
- in_weight: bfloat16 [768, 2304], P('fsdp'), may hold values from -0.21875 to 0.21875
- down_weight: bfloat16 [1152, 768], P(None, 'fsdp'), may hold values from -0.1875 to 0.1875
- cotangent: bfloat16 [8, 512, 768], P('fsdp', 'seq'), may hold values from -6 to 6
Outputs:
- block_out: bfloat16 [8, 512, 768], P('fsdp', 'seq')
- input_grad: bfloat16 [8, 512, 768], P('fsdp', 'seq')
- qkv_weight_grad: float32 [768, 2304], P('fsdp')
- out_weight_grad: float32 [768, 768], P('fsdp')
- in_weight_grad: float32 [768, 2304], P('fsdp')
- down_weight_grad: float32 [1152, 768], P(None, 'fsdp')
- norm1_gain_grad: float32 [768], P('fsdp')
- norm2_gain_grad: float32 [768], P('fsdp')
Inputs may be any that keep to these rules, and one draw needn't show every extreme that they name: Along each sequence the positions rise by 1 or 2 from one token to the next. `qkv_weight`: A projection matrix; every entry lies within 16 / sqrt(768) of zero.
All inputs are finite; a program needn't handle non-finite values.
Results may differ from a plain program's by a relative error of at most 0.019.
Values may be sent and summed in bfloat16 or wider, within the bound.
A program may use at most 128 MiB of HBM per device.

v0:
```python
import jax
import jax.numpy as jnp
from jax import lax
from jax.sharding import PartitionSpec as P

HEADS = 12
HEAD_DIM = 64
eps = 1e-05
theta = 160000.0


def layer_norm(values, gain_vec):
    middle = jnp.mean(values, axis=-1, keepdims=True)
    centred = values - middle
    inverse = lax.rsqrt(jnp.mean(centred * centred, axis=-1, keepdims=True) + eps)
    scaled = centred * inverse
    return (scaled * gain_vec, scaled, inverse)


def norm_back(upstream, scaled, inverse, gain_vec):
    gain_grad = jnp.sum(upstream * scaled, axis=0)
    weighted = upstream * gain_vec
    result = inverse * (
        weighted
        - jnp.mean(weighted, axis=-1, keepdims=True)
        - scaled * jnp.mean(weighted * scaled, axis=-1, keepdims=True)
    )
    return (result, gain_grad)


def rotary_tables(positions, head_size):
    half_dim = head_size // 2
    frequency = theta ** (-jnp.arange(half_dim, dtype=jnp.float32) / half_dim)
    angles = positions.astype(jnp.float32)[..., None] * frequency
    return (jnp.cos(angles)[..., None, :], jnp.sin(angles)[..., None, :])


def rotate(values, cosine_table, sine_table):
    half_dim = values.shape[-1] // 2
    first_half = values[..., :half_dim]
    second_half = values[..., half_dim:]
    return jnp.concatenate(
        [
            first_half * cosine_table - second_half * sine_table,
            second_half * cosine_table + first_half * sine_table,
        ],
        axis=-1,
    )


def rotate_back(values, cosine_table, sine_table):
    half_dim = values.shape[-1] // 2
    first_half = values[..., :half_dim]
    second_half = values[..., half_dim:]
    return jnp.concatenate(
        [
            first_half * cosine_table + second_half * sine_table,
            second_half * cosine_table - first_half * sine_table,
        ],
        axis=-1,
    )


def gelu_slope(values):
    return (
        0.5 * (1.0 + lax.erf(values * 0.7071067811865476))
        + values * jnp.exp(-0.5 * values * values) * 0.3989422804014327
    )


def local(
    tokens,
    positions,
    norm1_gain,
    qkv_weight,
    out_weight,
    norm2_gain,
    in_weight,
    down_weight,
    cotangent,
):
    f32 = jnp.float32
    low = jnp.bfloat16
    groups = lax.axis_size("seq")
    seq_dev, span_len, model_width = tokens.shape
    row_count = seq_dev * span_len
    local_heads = HEADS // groups
    group_width = local_heads * HEAD_DIM
    length = span_len * groups
    block_rows = min(512, length)
    block_count = length // block_rows
    score_scale = HEAD_DIM ** (-0.5)
    gathered = (
        lax.all_gather(qkv_weight, "fsdp", axis=0, tiled=True),
        lax.all_gather(out_weight, "fsdp", axis=0, tiled=True),
        lax.all_gather(in_weight, "fsdp", axis=0, tiled=True),
        lax.all_gather(down_weight, "fsdp", axis=1, tiled=True),
        lax.all_gather(norm1_gain, "fsdp", axis=0, tiled=True),
        lax.all_gather(norm2_gain, "fsdp", axis=0, tiled=True),
    )
    w_qkv, w_out, w_in, w_down, gain_one, gain_two = gathered
    gain_one = gain_one.astype(f32)
    gain_two = gain_two.astype(f32)
    inputs = tokens.reshape(row_count, model_width).astype(f32)
    normed_one, scaled_one, inverse_one = layer_norm(inputs, gain_one)
    normed_one = normed_one.astype(low)
    projected = jnp.dot(normed_one, w_qkv, preferred_element_type=f32).reshape(
        seq_dev, span_len, 3, HEADS, HEAD_DIM
    )
    cosine_table, sine_table = rotary_tables(positions, HEAD_DIM)
    queries = rotate(projected[:, :, 0], cosine_table, sine_table)
    key_part = rotate(projected[:, :, 1], cosine_table, sine_table)
    packed = jnp.stack([queries, key_part, projected[:, :, 2]], axis=2).astype(low)
    packed = packed.reshape(seq_dev, span_len, 3, groups, group_width)
    heads = lax.all_to_all(packed, "seq", split_axis=3, concat_axis=1, tiled=True)
    heads = heads.reshape(seq_dev, length, 3, local_heads, HEAD_DIM)
    query_rows = heads[:, :, 0]
    key_rows = heads[:, :, 1]
    value_rows = heads[:, :, 2]
    query_blocks = jnp.swapaxes(
        query_rows.reshape(seq_dev, block_count, block_rows, local_heads, HEAD_DIM), 0, 1
    )

    def attend(query_block):
        scores = (
            jnp.einsum("bqhd,bkhd->bhqk", query_block, key_rows, preferred_element_type=f32)
            * score_scale
        )
        totals = jax.nn.logsumexp(scores, axis=-1)
        probs_low = jnp.exp(scores - totals[..., None]).astype(low)
        result = jnp.einsum("bhqk,bkhd->bqhd", probs_low, value_rows, preferred_element_type=f32)
        return (result.astype(low), totals)

    attended, totals = lax.map(attend, query_blocks)
    attended = jnp.swapaxes(attended, 0, 1).reshape(seq_dev, length, local_heads, HEAD_DIM)
    outgoing = attended.reshape(seq_dev, length, 1, group_width)
    returned = lax.all_to_all(outgoing, "seq", split_axis=1, concat_axis=2, tiled=True)
    mixed_heads = returned.reshape(row_count, model_width)
    residual = inputs + jnp.dot(mixed_heads, w_out, preferred_element_type=f32)
    normed_two, scaled_two, inverse_two = layer_norm(residual, gain_two)
    normed_two = normed_two.astype(low)
    lifted = jnp.dot(normed_two, w_in, preferred_element_type=f32)
    ff_size = lifted.shape[1] // 2
    act_input = lifted[:, :ff_size]
    gate_part = lifted[:, ff_size:]
    activated = jax.nn.gelu(act_input, approximate=False)
    gated = (activated * gate_part).astype(low)
    block_out = (residual + jnp.dot(gated, w_down, preferred_element_type=f32)).astype(low)
    regathered = (
        lax.all_gather(qkv_weight, "fsdp", axis=0, tiled=True),
        lax.all_gather(out_weight, "fsdp", axis=0, tiled=True),
        lax.all_gather(in_weight, "fsdp", axis=0, tiled=True),
        lax.all_gather(down_weight, "fsdp", axis=1, tiled=True),
        lax.all_gather(norm1_gain, "fsdp", axis=0, tiled=True),
        lax.all_gather(norm2_gain, "fsdp", axis=0, tiled=True),
    )
    w_qkv, w_out, w_in, w_down, gain_low_one, gain_low_two = regathered
    gain_one = gain_low_one.astype(f32)
    gain_two = gain_low_two.astype(f32)
    upstream = cotangent.reshape(row_count, model_width)
    gated_grad = jnp.dot(upstream, w_down.T, preferred_element_type=f32)
    lifted_grad = jnp.concatenate(
        [gated_grad * gate_part * gelu_slope(act_input), gated_grad * activated], axis=1
    ).astype(low)
    normed_two_grad = jnp.dot(lifted_grad, w_in.T, preferred_element_type=f32)
    residual_part, gain_two_grad = norm_back(normed_two_grad, scaled_two, inverse_two, gain_two)
    residual_grad = upstream.astype(f32) + residual_part
    residual_low = residual_grad.astype(low)
    mixed_grad = jnp.dot(residual_low, w_out.T, preferred_element_type=f32).astype(low)
    grad_outgoing = mixed_grad.reshape(seq_dev, span_len, groups, group_width)
    grad_heads = lax.all_to_all(grad_outgoing, "seq", split_axis=2, concat_axis=1, tiled=True)
    grad_heads = grad_heads.reshape(seq_dev, length, local_heads, HEAD_DIM)
    delta_rows = jnp.sum(grad_heads.astype(f32) * attended.astype(f32), axis=-1)
    grad_blocks = jnp.swapaxes(
        grad_heads.reshape(seq_dev, block_count, block_rows, local_heads, HEAD_DIM), 0, 1
    )
    delta_blocks = jnp.swapaxes(
        jnp.swapaxes(delta_rows.reshape(seq_dev, block_count, block_rows, local_heads), 0, 1), 2, 3
    )

    def attend_back(carry, block_inputs):
        key_total, value_total = carry
        query_block, grad_block, delta_block, total_block = block_inputs
        scores = (
            jnp.einsum("bqhd,bkhd->bhqk", query_block, key_rows, preferred_element_type=f32)
            * score_scale
        )
        probs = jnp.exp(scores - total_block[..., None])
        probs_low = probs.astype(low)
        value_total = value_total + jnp.einsum(
            "bhqk,bqhd->bkhd", probs_low, grad_block, preferred_element_type=f32
        )
        prob_grad = jnp.einsum(
            "bqhd,bkhd->bhqk", grad_block, value_rows, preferred_element_type=f32
        )
        score_grad = (probs * (prob_grad - delta_block[..., None])).astype(low)
        query_grad = (
            jnp.einsum("bhqk,bkhd->bqhd", score_grad, key_rows, preferred_element_type=f32)
            * score_scale
        ).astype(low)
        key_total = key_total + jnp.einsum(
            "bhqk,bqhd->bkhd", score_grad, query_block, preferred_element_type=f32
        )
        return ((key_total, value_total), query_grad)

    zeros_state = jnp.zeros((seq_dev, length, local_heads, HEAD_DIM), f32)
    (key_total, value_total), query_grads = lax.scan(
        attend_back, (zeros_state, zeros_state), (query_blocks, grad_blocks, delta_blocks, totals)
    )
    query_grad = jnp.swapaxes(query_grads, 0, 1).reshape(seq_dev, length, group_width)
    key_grad = (key_total * score_scale).astype(low).reshape(seq_dev, length, group_width)
    value_grad = value_total.astype(low).reshape(seq_dev, length, group_width)
    grads_outgoing = jnp.stack([query_grad, key_grad, value_grad], axis=2)[:, :, :, None, :]
    grads_returned = lax.all_to_all(grads_outgoing, "seq", split_axis=1, concat_axis=3, tiled=True)
    grads_returned = grads_returned.reshape(seq_dev, span_len, 3, HEADS, HEAD_DIM).astype(f32)
    qkv_grad = jnp.stack(
        [
            rotate_back(grads_returned[:, :, 0], cosine_table, sine_table),
            rotate_back(grads_returned[:, :, 1], cosine_table, sine_table),
            grads_returned[:, :, 2],
        ],
        axis=2,
    )
    qkv_grad = qkv_grad.reshape(row_count, 3 * model_width).astype(low)
    normed_one_grad = jnp.dot(qkv_grad, w_qkv.T, preferred_element_type=f32)
    input_part, gain_one_grad = norm_back(normed_one_grad, scaled_one, inverse_one, gain_one)
    input_grad = (residual_grad + input_part).astype(low).reshape(seq_dev, span_len, model_width)
    gain_terms = (gain_one_grad, gain_two_grad)
    terms = (
        jnp.dot(normed_one.T, qkv_grad, preferred_element_type=f32),
        jnp.dot(mixed_heads.T, residual_low, preferred_element_type=f32),
        jnp.dot(normed_two.T, lifted_grad, preferred_element_type=f32),
        jnp.dot(gated.T, upstream, preferred_element_type=f32),
        gain_terms[0],
        gain_terms[1],
    )
    pieces = (
        lax.psum_scatter(terms[0], "fsdp", scatter_dimension=0, tiled=True),
        lax.psum_scatter(terms[1], "fsdp", scatter_dimension=0, tiled=True),
        lax.psum_scatter(terms[2], "fsdp", scatter_dimension=0, tiled=True),
        lax.psum_scatter(terms[3], "fsdp", scatter_dimension=1, tiled=True),
        lax.psum_scatter(terms[4], "fsdp", scatter_dimension=0, tiled=True),
        lax.psum_scatter(terms[5], "fsdp", scatter_dimension=0, tiled=True),
    )
    parts = (
        lax.psum_scatter(
            pieces[0].astype(jnp.bfloat16), "seq", scatter_dimension=0, tiled=True
        ).astype(jnp.float32),
        lax.psum_scatter(
            pieces[1].astype(jnp.bfloat16), "seq", scatter_dimension=0, tiled=True
        ).astype(jnp.float32),
        lax.psum_scatter(
            pieces[2].astype(jnp.bfloat16), "seq", scatter_dimension=0, tiled=True
        ).astype(jnp.float32),
        lax.psum_scatter(
            pieces[3].astype(jnp.bfloat16), "seq", scatter_dimension=1, tiled=True
        ).astype(jnp.float32),
        lax.psum_scatter(
            pieces[4].astype(jnp.bfloat16), "seq", scatter_dimension=0, tiled=True
        ).astype(jnp.float32),
        lax.psum_scatter(
            pieces[5].astype(jnp.bfloat16), "seq", scatter_dimension=0, tiled=True
        ).astype(jnp.float32),
    )
    summed = (
        lax.all_gather(parts[0].astype(jnp.bfloat16), "seq", axis=0, tiled=True).astype(
            jnp.float32
        ),
        lax.all_gather(parts[1].astype(jnp.bfloat16), "seq", axis=0, tiled=True).astype(
            jnp.float32
        ),
        lax.all_gather(parts[2].astype(jnp.bfloat16), "seq", axis=0, tiled=True).astype(
            jnp.float32
        ),
        lax.all_gather(parts[3].astype(jnp.bfloat16), "seq", axis=1, tiled=True).astype(
            jnp.float32
        ),
        lax.all_gather(parts[4].astype(jnp.bfloat16), "seq", axis=0, tiled=True).astype(
            jnp.float32
        ),
        lax.all_gather(parts[5].astype(jnp.bfloat16), "seq", axis=0, tiled=True).astype(
            jnp.float32
        ),
    )
    return (
        block_out.reshape(seq_dev, span_len, model_width),
        input_grad,
        summed[0],
        summed[1],
        summed[2],
        summed[3],
        summed[4],
        summed[5],
    )


def solution(mesh):
    in_specs = (
        P("fsdp", "seq", None),
        P("fsdp", "seq"),
        P("fsdp"),
        P("fsdp", None),
        P("fsdp", None),
        P("fsdp"),
        P("fsdp", None),
        P(None, "fsdp"),
        P("fsdp", "seq", None),
    )
    out_specs = (
        P("fsdp", "seq", None),
        P("fsdp", "seq", None),
        P("fsdp", None),
        P("fsdp", None),
        P("fsdp", None),
        P(None, "fsdp"),
        P("fsdp"),
        P("fsdp"),
    )
    return jax.shard_map(local, mesh=mesh, in_specs=in_specs, out_specs=out_specs, check_vma=False)
```

profile of v0, /device:TPU:0, one launch (start us, length us, event | category | flops | bytes accessed | tf_op | source)
XLA Modules:
  0.0 489.6 jit_solution(12036840399194156989)
XLA Ops:
  9.4 1.3 fusion.60
  13.1 16.1 %all-reduce.10 = (bf16[768]{0:T(1024)(128)(2,1)S(1)}, bf16[768]{0:T(1024)(128)(2,1)}) all-reduce(bf16[768]{0:T(1024)(128)(2,1)S(1)} %dynamic-update-slice, bf16[768]{0:T(1024)(128)(2,1)S(1)} %dynamic-update-slice.1), channel_id=1, replica_groups=mesh['seq'=4,'fsdp'=8] {'fsdp'}, use_global_device_ids=true, to_apply=%add | all-reduce | flops 1536 | bytes 6144
  32.8 13.7 %all-gather.5.cloned.1.call-done = bf16[768,2304]{1,0:T(8,128)(2,1)} async-done(((bf16[96,2304]{1,0:T(8,128)(2,1)}), bf16[768,2304]{1,0:T(8,128)(2,1)}) %all-gather.5.cloned.1.call-update) | async-done | bytes 3538960 | tf_op jit(solution)/shard_map/all_gather | solution.py:94
  46.6 4.5 copy.88
  51.1 2.1 convolution_bitcast_fusion
  54.4 4.6 all-to-all-start
  59.6 15.7 %all-to-all-done = bf16[1,128,3,4,192]{1,4,2,0,3:T(8,128)(2,1)S(1)} async-done(((bf16[1,128,3,4,192]{1,4,2,0,3:T(8,128)(2,1)}), bf16[1,128,3,4,192]{1,4,2,0,3:T(8,128)(2,1)S(1)}, u32[]{:S(2)}, u32[]{:S(2)}) %all-to-all-start) | async-done | bytes 589856 | tf_op jit(solution)/shard_map/all_to_all | solution.py:115
  76.8 1.7 multiply_reduce_fusion
  79.0 1.6 convolution_convert_fusion.2
  82.2 3.9 reduce.6
  86.1 2.0 reshape.502
  88.1 3.4 all-to-all-start.1
  92.4 6.4 %all-to-all-done.1 = bf16[4,2,12288]{2,1,0:T(2,128)(2,1)S(1)} async-done(((bf16[4,2,12288]{2,1,0:T(2,128)(2,1)}), bf16[4,2,12288]{2,1,0:T(2,128)(2,1)S(1)}, u32[]{:S(2)}, u32[]{:S(2)}) %all-to-all-start.1) | async-done | bytes 196640 | tf_op jit(solution)/shard_map/all_to_all | solution.py:137
  99.8 1.9 copy.95
  103.3 1.8 fusion.62
  106.5 1.7 all-gather.9.cloned.1.call-done
  108.1 3.7 fusion.58
  111.9 24.5 %all-gather.11.cloned.1.call-done = bf16[1152,768]{0,1:T(8,128)(2,1)} async-done(((bf16[1152,96]{0,1:T(8,128)(2,1)}), bf16[1152,768]{0,1:T(8,128)(2,1)}) %all-gather.11.cloned.1.call-update) | async-done | bytes 1769488 | tf_op jit(solution)/shard_map/all_gather | solution.py:97
  136.3 4.6 multiply_convert_fusion.1
  141.0 1.9 multiply_reduce_fusion.1
  143.9 1.9 fusion.49
  147.9 3.3 fusion.42
  151.3 5.2 %fusion.36 = f32[768,2304]{1,0:T(8,128)} fusion(bf16[128,1152]{1,0:T(8,128)(2,1)} %copy-done.13, bf16[128,1152]{1,0:T(8,128)(2,1)} %copy-done.14, f32[128,768]{1,0:T(8,128)S(1)} %get-tuple-element.98, f32[768]{0:T(1024)S(1)} %convert_element_type.222, f32[128]{0:T(128)} %add_rsqrt_fusion, f32[128]{0:T(128)} %copy-done.21), kind=kOutput, calls=%fused_computation.80 | convolution fusion | flops 454557696 | bytes 8065024 | tf_op jit(solution)/shard_map/dot_general | solution.py:232
  156.5 2.7 convolution_convert_fusion.1
  159.2 1.7 copy.97
  161.0 12.5 %all_to_all.54 = bf16[1,128,4,192]{1,3,0,2:T(8,128)(2,1)S(1)} all-to-all(bf16[1,128,4,192]{1,3,0,2:T(8,128)(2,1)} %bitcast.196), channel_id=1, replica_groups=mesh['seq'=4,'fsdp'=8] {'seq'}, dimensions={2} | all-to-all | bytes 393216 | tf_op jit(solution)/shard_map/all_to_all | solution.py:171
  175.0 1.7 reshape.470
  178.6 1.9 reshape.473
  181.7 1.9 multiply_convert_fusion
  186.1 28.2 %all_to_all.55 = bf16[1,512,3,1,192]{4,2,3,0,1:T(4,128)(2,1)S(1)} all-to-all(bf16[1,512,3,1,192]{4,2,3,0,1:T(4,128)(2,1)S(1)} %copy.105), channel_id=1, replica_groups=mesh['seq'=4,'fsdp'=8] {'seq'}, dimensions={1} | all-to-all | bytes 1179648 | tf_op jit(solution)/shard_map/all_to_all | solution.py:214
  216.3 4.2 fusion.46
  220.6 1.8 convert_element_type.251
  222.5 17.1 %reduce-scatter.23.cloned.1.call-done = f32[1152,96]{0,1:T(8,128)} async-done(((f32[1152,768]{0,1:T(8,128)}), f32[1152,96]{0,1:T(8,128)}) %reduce-scatter.23.cloned.1.call-update) | async-done | bytes 442384 | tf_op jit(solution)/shard_map/reduce_scatter | solution.py:241
  239.6 1.7 convert_element_type.255
  241.4 67.3 %reduce-scatter.19.cloned.1.call-done = f32[96,2304]{1,0:T(8,128)} async-done(((f32[768,2304]{1,0:T(8,128)}), f32[96,2304]{1,0:T(8,128)}) %reduce-scatter.19.cloned.1.call-update) | async-done | bytes 884752 | tf_op jit(solution)/shard_map/reduce_scatter | solution.py:240
  308.7 2.0 convert_element_type.253
  312.6 1.3 fusion.4
  313.9 3.4 fusion.31
  317.4 60.3 %reduce-scatter.11.cloned.1.call-done = f32[96,2304]{1,0:T(8,128)} async-done(((f32[768,2304]{1,0:T(8,128)}), f32[96,2304]{1,0:T(8,128)}) %reduce-scatter.11.cloned.1.call-update) | async-done | bytes 884752 | tf_op jit(solution)/shard_map/reduce_scatter | solution.py:238
  377.7 2.0 convert_element_type.249
  379.7 12.8 %all-reduce.9 = (bf16[768]{0:T(1024)(128)(2,1)S(1)}, bf16[768]{0:T(1024)(128)(2,1)S(1)}) all-reduce(f32[768]{0:T(1024)S(1)} %get-tuple-element.48, f32[768]{0:T(1024)S(1)} %copy-done.26), channel_id=10, replica_groups=mesh['seq'=4,'fsdp'=8] {'fsdp'}, use_global_device_ids=true, to_apply=%region_20.21.clone | all-reduce | flops 1536 | bytes 9216
  392.6 11.7 %all-reduce.12 = (bf16[96]{0:T(256)(128)(2,1)S(1)}, bf16[96]{0:T(256)(128)(2,1)S(1)}) all-reduce(bf16[96]{0:T(256)(128)(2,1)S(1)} %dynamic-slice.19, bf16[96]{0:T(256)(128)(2,1)S(1)} %dynamic-slice.18), channel_id=11, replica_groups=mesh['seq'=4,'fsdp'=8] {'seq'}, use_global_device_ids=true, to_apply=%region_21.22.clone | all-reduce | flops 192 | bytes 768
  404.9 8.3 %all-reduce.11 = (bf16[96]{0:T(256)(128)(2,1)S(1)}, bf16[96]{0:T(256)(128)(2,1)S(1)}) all-reduce(bf16[96]{0:T(256)(128)(2,1)S(1)} %dynamic-update-slice.2, bf16[96]{0:T(256)(128)(2,1)S(1)} %dynamic-update-slice.3), channel_id=1, replica_groups=mesh['seq'=4,'fsdp'=8] {'seq'}, use_global_device_ids=true, to_apply=%add.2 | all-reduce | flops 192 | bytes 768
  415.1 13.9 %all_gather.49 = bf16[96,768]{1,0:T(8,128)(2,1)S(1)} all-gather(bf16[24,768]{1,0:T(8,128)(2,1)} %reduce-scatter.17.cloned.1.call-done), channel_id=1, replica_groups=mesh['seq'=4,'fsdp'=8] {'seq'}, dimensions={0}, use_global_device_ids=true | all-gather | bytes 184320 | tf_op jit(solution)/shard_map/all_gather | solution.py:269
  429.7 14.9 %all_gather.51 = bf16[1152,96]{0,1:T(8,128)(2,1)S(1)} all-gather(bf16[1152,24]{0,1:T(8,128)(2,1)} %reduce-scatter.25.cloned.1.call-done), channel_id=1, replica_groups=mesh['seq'=4,'fsdp'=8] {'seq'}, dimensions={1}, use_global_device_ids=true | all-gather | bytes 276480 | tf_op jit(solution)/shard_map/all_gather | solution.py:275
  445.4 17.3 %all_gather.50 = bf16[96,2304]{1,0:T(8,128)(2,1)S(1)} all-gather(bf16[24,2304]{1,0:T(8,128)(2,1)} %reduce-scatter.21.cloned.1.call-done), channel_id=1, replica_groups=mesh['seq'=4,'fsdp'=8] {'seq'}, dimensions={0}, use_global_device_ids=true | all-gather | bytes 552960 | tf_op jit(solution)/shard_map/all_gather | solution.py:272
  463.7 2.5 reduce-scatter.13.cloned.1.call-done
  466.2 15.6 %all_gather.48 = bf16[96,2304]{1,0:T(8,128)(2,1)S(1)} all-gather(bf16[24,2304]{1,0:T(8,128)(2,1)} %reduce-scatter.13.cloned.1.call-done), channel_id=1, replica_groups=mesh['seq'=4,'fsdp'=8] {'seq'}, dimensions={0}, use_global_device_ids=true | all-gather | bytes 552960 | tf_op jit(solution)/shard_map/all_gather | solution.py:266
  (154 shorter events, 36.3 us)
Async XLA Ops:
  7.2 39.4 %all-gather.5.cloned.1.call-start = ((), (), s32[]{:S(2)}) async-start(), calls=%async_computation.12 | async-start | bytes 3981312 | tf_op jit(solution)/shard_map/all_gather | solution.py:94
  7.9 95.4 %all-gather.7.cloned.1.call-start = ((), (), s32[]{:S(2)}) async-start(), calls=%async_computation.13 | async-start | bytes 1327104 | tf_op jit(solution)/shard_map/all_gather | solution.py:95
  8.6 99.5 %all-gather.9.cloned.1.call-start = ((), (), s32[]{:S(2)}) async-start(), calls=%async_computation.14 | async-start | bytes 3981312 | tf_op jit(solution)/shard_map/all_gather | solution.py:96
  30.2 20.8 %copy-start.19 = (f32[128]{0:T(128)}, f32[128]{0:T(128)S(1)}, u32[]{:S(2)}) copy-start(f32[128]{0:T(128)S(1)} %broadcast_multiply_fusion.5) | copy-start | bytes 1540
  31.4 19.7 %copy-start.23 = (f32[128]{0:T(128)}, f32[128]{0:T(128)S(1)}, u32[]{:S(2)}) copy-start(f32[128]{0:T(128)S(1)} %add_rsqrt_fusion.1) | copy-start | bytes 1540
  51.1 2.3 copy-start.15
  51.1 2.3 copy-start.17
  54.4 20.9 %all-to-all-start = ((bf16[1,128,3,4,192]{1,4,2,0,3:T(8,128)(2,1)}), bf16[1,128,3,4,192]{1,4,2,0,3:T(8,128)(2,1)S(1)}, u32[]{:S(2)}, u32[]{:S(2)}) async-start(bf16[1,128,3,4,192]{1,4,2,0,3:T(8,128)(2,1)} %pad_maximum_fusion), calls=%async_computation | async-start | bytes 1179648 | tf_op jit(solution)/shard_map/all_to_all | solution.py:115
  59.0 77.3 %all-gather.11.cloned.1.call-start = ((), (), s32[]{:S(2)}) async-start(), calls=%async_computation.15 | async-start | bytes 1990656 | tf_op jit(solution)/shard_map/all_gather | solution.py:97
  80.6 22.7 %copy-start.9 = (bf16[3,64,512]{2,1,0:T(8,128)(2,1)}, bf16[3,64,512]{2,1,0:T(8,128)(2,1)S(1)}, u32[]{:S(2)}) copy-start(bf16[3,64,512]{2,1,0:T(8,128)(2,1)S(1)} %convolution_convert_fusion.2) | copy-start | bytes 589828
  88.1 10.6 %all-to-all-start.1 = ((bf16[4,2,12288]{2,1,0:T(2,128)(2,1)}), bf16[4,2,12288]{2,1,0:T(2,128)(2,1)S(1)}, u32[]{:S(2)}, u32[]{:S(2)}) async-start(bf16[4,2,12288]{2,1,0:T(2,128)(2,1)} %reshape.502), calls=%async_computation.1 | async-start | bytes 393216 | tf_op jit(solution)/shard_map/all_to_all | solution.py:137
  91.5 129.1 %reduce-scatter.15.cloned.1.call-start = ((), (), s32[]{:S(2)}) async-start(), calls=%async_computation.18 | async-start | bytes 2654208 | tf_op jit(solution)/shard_map/reduce_scatter | solution.py:239
  105.2 0.6 copy-start.21
  136.3 4.6 copy-start.4
  136.3 4.6 copy-start.22
  136.3 4.6 copy-start.25
  140.9 2.2 copy-start.13
  140.9 2.2 copy-start.14
  140.9 2.0 copy-start.12
  141.0 2.9 copy-start.8
  143.1 0.7 copy-start.1
  145.8 93.8 %reduce-scatter.23.cloned.1.call-start = ((), (), s32[]{:S(2)}) async-start(), calls=%async_computation.22 | async-start | bytes 3981312 | tf_op jit(solution)/shard_map/reduce_scatter | solution.py:241
  147.2 0.7 copy-start.5
  151.2 157.4 %reduce-scatter.19.cloned.1.call-start = ((), (), s32[]{:S(2)}) async-start(), calls=%async_computation.20 | async-start | bytes 7962624 | tf_op jit(solution)/shard_map/reduce_scatter | solution.py:240
  156.5 221.2 %reduce-scatter.11.cloned.1.call-start = ((), (), s32[]{:S(2)}) async-start(), calls=%async_computation.16 | async-start | bytes 7962624 | tf_op jit(solution)/shard_map/reduce_scatter | solution.py:238
  173.5 0.7 copy-start.10
  180.5 3.1 copy-start.3
  183.7 1.0 copy-start.7
  215.2 0.7 copy-start.16
  215.3 0.7 copy-start.18
  215.4 0.9 copy-start
  215.4 0.9 copy-start.20
  215.4 0.9 copy-start.24
  220.5 92.1 %copy-start.6 = (bf16[128,1152]{1,0:T(8,128)(2,1)S(1)}, bf16[128,1152]{1,0:T(8,128)(2,1)}, u32[]{:S(2)}) copy-start(bf16[128,1152]{1,0:T(8,128)(2,1)} %copy-done.5) | copy-start | bytes 884740
  220.5 92.1 %copy-start.11 = (bf16[1152,768]{0,1:T(8,128)(2,1)S(1)}, bf16[1152,768]{0,1:T(8,128)(2,1)}, u32[]{:S(2)}) copy-start(bf16[1152,768]{0,1:T(8,128)(2,1)} %all-gather.11.cloned.1.call-done) | copy-start | bytes 5308420
  220.5 194.6 %reduce-scatter.17.cloned.1.call-start = ((), (), s32[]{:S(2)}) async-start(), calls=%async_computation.19 | async-start | bytes 184320 | tf_op jit(solution)/shard_map/reduce_scatter | solution.py:249
  222.4 207.3 %reduce-scatter.25.cloned.1.call-start = ((), (), s32[]{:S(2)}) async-start(), calls=%async_computation.23 | async-start | bytes 276480
  241.3 204.1 %reduce-scatter.21.cloned.1.call-start = ((), (), s32[]{:S(2)}) async-start(), calls=%async_computation.21 | async-start | bytes 552960 | tf_op jit(solution)/shard_map/reduce_scatter | solution.py:252
  310.7 155.6 %reduce-scatter.13.cloned.1.call-start = ((), (), s32[]{:S(2)}) async-start(), calls=%async_computation.17 | async-start | bytes 552960 | tf_op jit(solution)/shard_map/reduce_scatter | solution.py:246
  313.9 65.8 %copy-start.26 = (f32[768]{0:T(1024)S(1)}, f32[768]{0:T(1024)}, u32[]{:S(2)}) copy-start(f32[768]{0:T(1024)} %get-tuple-element.46) | copy-start | bytes 9220
  313.9 100.3 %copy-start.2 = (f32[128,768]{1,0:T(8,128)S(1)}, f32[128,768]{1,0:T(8,128)}, u32[]{:S(2)}) copy-start(f32[128,768]{1,0:T(8,128)} %copy-done.1) | copy-start | bytes 1179652
Sparse Core Ops, SparseCore 0:
  9.9 36.6 all-gather.4
  48.4 23.9 all-gather.6
  74.3 33.8 all-gather.8
  109.9 26.3 all-gather.10
  145.9 42.3 reduce-scatter.14
  191.6 47.9 reduce-scatter.22
  243.1 65.4 reduce-scatter.18
  312.2 65.4 reduce-scatter.10
  379.9 19.4 reduce-scatter.16
  401.6 17.8 reduce-scatter.24
  422.4 21.0 reduce-scatter.20
  446.2 19.9 reduce-scatter.12
where the time goes:
time: 491 us; the launch traced here: 490 us
  waiting for transfers between devices  212 us (43%)
  blocking collectives  151 us (31%)
  matrix products  43 us (9%)
  local copies, waits for them, and re-layouts  30.4 us (6%)
  other arithmetic  27.2 us (6%)
  between operations  17.3 us (4%)
  starting transfers between devices  8.59 us (2%)
    reduce_scatter x1, waiting for transfers between devices, local(): lax.psum_scatter(terms[2], 'fsdp', scatter_dimension=0, tiled=True)  67.3 us
    reduce_scatter x1, waiting for transfers between devices, local(): lax.psum_scatter(terms[0], 'fsdp', scatter_dimension=0, tiled=True)  60.3 us
    unnamed x4, blocking collectives  48.9 us
    all_to_all x1, blocking collectives, local(): lax.all_to_all(grads_outgoing, 'seq', split_axis=1, concat_axis=3, tiled=...  28.2 us
    all_gather x1, waiting for transfers between devices, local(): lax.all_gather(down_weight, 'fsdp', axis=1, tiled=True)  24.5 us
    all_gather x1, blocking collectives, local(): lax.all_gather(parts[2].astype(jnp.bfloat16), 'seq', axis=0, tiled=True)  17.3 us
    reduce_scatter x1, waiting for transfers between devices, local(): lax.psum_scatter(terms[3], 'fsdp', scatter_dimension=1, tiled=True)  17.1 us
    all_to_all x1, waiting for transfers between devices, local(): lax.all_to_all(packed, 'seq', split_axis=3, concat_axis=1, tiled=True)  15.7 us
  transfers between devices with their start and end apart: 14, of which 9 were waited for; matrix products, arithmetic and copies ran while one was open for 18% of the time, Pallas kernels for 0%

commit v1 on v0

--- a/solution.py
+++ b/solution.py
@@ -7,6 +7,17 @@
 HEAD_DIM = 64
 eps = 1e-05
 theta = 160000.0
+
+
+def in_blocks(x, dim, devices):
+    before, after = (x.shape[:dim], x.shape[dim + 1 :])
+    return jnp.moveaxis(x.reshape(*before, devices, -1, *after), dim, 0)
+
+
+def in_order(pieces, dim):
+    pieces = jnp.moveaxis(pieces, 0, dim)
+    dims = pieces.shape
+    return pieces.reshape(*dims[:dim], dims[dim] * dims[dim + 1], *dims[dim + 2 :])
 
 
 def layer_norm(values, gain_vec):
@@ -211,7 +222,15 @@
     key_grad = (key_total * score_scale).astype(low).reshape(seq_dev, length, group_width)
     value_grad = value_total.astype(low).reshape(seq_dev, length, group_width)
     grads_outgoing = jnp.stack([query_grad, key_grad, value_grad], axis=2)[:, :, :, None, :]
-    grads_returned = lax.all_to_all(grads_outgoing, "seq", split_axis=1, concat_axis=3, tiled=True)
+    length_2, index = (lax.axis_size("seq"), lax.axis_index("seq"))
+    blocks = in_blocks(grads_outgoing, 1, length_2)
+    whole = blocks
+    for hop in range(1, length_2):
+        target, source = ((index + hop) % length_2, (index - hop) % length_2)
+        sent = lax.dynamic_index_in_dim(blocks, target, 0)
+        other = lax.ppermute(sent, "seq", [(i, (i + hop) % length_2) for i in range(length_2)])
+        whole = lax.dynamic_update_slice_in_dim(whole, other, source, axis=0)
+    grads_returned = in_order(whole, 3)
     grads_returned = grads_returned.reshape(seq_dev, span_len, 3, HEADS, HEAD_DIM).astype(f32)
     qkv_grad = jnp.stack(
         [

time: 491 us -> 491 us (level)
  blocking collectives: 151 us -> 111 us
  waiting for transfers between devices: 212 us -> 236 us
  local copies, waits for them, and re-layouts: 30.4 us -> 36.3 us
  starting transfers between devices: 8.59 us -> 14.1 us
  matrix products: 43 us -> 48.5 us
    all_to_all x2 -> x0, blocking collectives: 40.7 us -> none  [the longest x1 28.2 us: local(): lax.all_to_all(grads_outgoing, 'seq', split_axis=1, concat_axis=3, tiled=...]
    ppermute x0 -> x3, waiting for transfers between devices: none -> 13.9 us  [local(): lax.ppermute(sent, 'seq', [(i, (i + hop) % length_2) for i in range(lengt...]
    all_to_all x0 -> x1, waiting for transfers between devices: none -> 8.02 us  [local(): lax.all_to_all(grad_outgoing, 'seq', split_axis=2, concat_axis=1, tiled=T...]
    unnamed x70 -> x68, local copies, waits for them, and re-layouts: 10.6 us -> 13 us
  transfers between devices with their start and end apart: 14 -> 18, of which waited for: 9 -> 12; matrix products, arithmetic and copies ran while one was open for 18% -> 20% of each run, Pallas kernels for 0% -> 0%
where the time goes in v1:
time: 491 us; the launch traced here: 490 us
  waiting for transfers between devices  236 us (48%)
  blocking collectives  111 us (23%)
  matrix products  48.5 us (10%)
  local copies, waits for them, and re-layouts  36.3 us (7%)
  other arithmetic  27.2 us (6%)
  between operations  17.4 us (4%)
  starting transfers between devices  14.1 us (3%)
    reduce_scatter x1, waiting for transfers between devices, local(): lax.psum_scatter(terms[2], 'fsdp', scatter_dimension=0, tiled=True)  67.2 us
    reduce_scatter x1, waiting for transfers between devices, local(): lax.psum_scatter(terms[0], 'fsdp', scatter_dimension=0, tiled=True)  60.3 us
    unnamed x4, blocking collectives  48.9 us
    all_gather x1, waiting for transfers between devices, local(): lax.all_gather(down_weight, 'fsdp', axis=1, tiled=True)  24.4 us
    reduce_scatter x1, waiting for transfers between devices, local(): lax.psum_scatter(terms[3], 'fsdp', scatter_dimension=1, tiled=True)  19 us
    all_gather x1, blocking collectives, local(): lax.all_gather(parts[2].astype(jnp.bfloat16), 'seq', axis=0, tiled=True)  17.3 us
    all_to_all x1, waiting for transfers between devices, local(): lax.all_to_all(packed, 'seq', split_axis=3, concat_axis=1, tiled=True)  15.7 us
    all_gather x1, blocking collectives, local(): lax.all_gather(parts[0].astype(jnp.bfloat16), 'seq', axis=0, tiled=True)  15.6 us
  transfers between devices with their start and end apart: 18, of which 12 were waited for; matrix products, arithmetic and copies ran while one was open for 20% of the time, Pallas kernels for 0%

profile of v1, /device:TPU:0, one launch (start us, length us, event | category | flops | bytes accessed | tf_op | source)
XLA Modules:
  0.0 489.8 jit_solution(17406953737559331755)
XLA Ops:
  13.1 16.1 %all-reduce.10 = (bf16[768]{0:T(1024)(128)(2,1)S(1)}, bf16[768]{0:T(1024)(128)(2,1)}) all-reduce(bf16[768]{0:T(1024)(128)(2,1)S(1)} %dynamic-update-slice, bf16[768]{0:T(1024)(128)(2,1)S(1)} %dynamic-update-slice.1), channel_id=1, replica_groups=mesh['seq'=4,'fsdp'=8] {'fsdp'}, use_global_device_ids=true, to_apply=%add | all-reduce | flops 1536 | bytes 6144
  32.8 13.7 %all-gather.5.cloned.1.call-done = bf16[768,2304]{1,0:T(8,128)(2,1)} async-done(((bf16[96,2304]{1,0:T(8,128)(2,1)}), bf16[768,2304]{1,0:T(8,128)(2,1)}) %all-gather.5.cloned.1.call-update) | async-done | bytes 3538960 | tf_op jit(solution)/shard_map/all_gather | solution.py:105
  46.6 4.5 copy.55
  51.1 2.1 convolution_bitcast_fusion
  54.4 4.6 all-to-all-start
  59.6 15.7 %all-to-all-done = bf16[1,128,3,4,192]{1,4,2,0,3:T(8,128)(2,1)S(1)} async-done(((bf16[1,128,3,4,192]{1,4,2,0,3:T(8,128)(2,1)}), bf16[1,128,3,4,192]{1,4,2,0,3:T(8,128)(2,1)S(1)}, u32[]{:S(2)}, u32[]{:S(2)}) %all-to-all-start) | async-done | bytes 589856 | tf_op jit(solution)/shard_map/all_to_all | solution.py:126
  82.2 3.9 reduce.6
  86.1 2.0 reshape.503
  88.1 3.4 all-to-all-start.1
  92.4 6.4 %all-to-all-done.1 = bf16[4,2,12288]{2,1,0:T(2,128)(2,1)S(1)} async-done(((bf16[4,2,12288]{2,1,0:T(2,128)(2,1)}), bf16[4,2,12288]{2,1,0:T(2,128)(2,1)S(1)}, u32[]{:S(2)}, u32[]{:S(2)}) %all-to-all-start.1) | async-done | bytes 196640 | tf_op jit(solution)/shard_map/all_to_all | solution.py:148
  99.8 1.9 copy.62
  103.3 1.8 fusion.65
  106.4 1.8 all-gather.9.cloned.1.call-done
  108.2 3.7 fusion.61
  111.9 24.4 %all-gather.11.cloned.1.call-done = bf16[1152,768]{0,1:T(8,128)(2,1)} async-done(((bf16[1152,96]{0,1:T(8,128)(2,1)}), bf16[1152,768]{0,1:T(8,128)(2,1)}) %all-gather.11.cloned.1.call-update) | async-done | bytes 1769488 | tf_op jit(solution)/shard_map/all_gather | solution.py:108
  136.3 4.6 multiply_convert_fusion.1
  141.0 1.9 multiply_reduce_fusion.1
  143.9 1.9 fusion.52
  147.9 3.3 fusion.45
  151.3 5.2 %fusion.39 = f32[768,2304]{1,0:T(8,128)} fusion(bf16[128,1152]{1,0:T(8,128)(2,1)} %copy-done.11, bf16[128,1152]{1,0:T(8,128)(2,1)} %copy-done.12, f32[128,768]{1,0:T(8,128)S(1)} %get-tuple-element.101, f32[768]{0:T(1024)S(1)} %convert_element_type.219, f32[128]{0:T(128)} %add_rsqrt_fusion, f32[128]{0:T(128)} %copy-done.19), kind=kOutput, calls=%fused_computation.82 | convolution fusion | flops 454557696 | bytes 8065024 | tf_op jit(solution)/shard_map/dot_general | solution.py:251
  156.5 2.7 convolution_convert_fusion.1
  159.2 1.7 copy.64
  161.0 4.6 all-to-all-start.2
  165.6 8.0 %all-to-all-done.2 = bf16[1,128,4,192]{1,3,0,2:T(8,128)(2,1)} async-done(((bf16[1,128,4,192]{1,3,0,2:T(8,128)(2,1)}), bf16[1,128,4,192]{1,3,0,2:T(8,128)(2,1)}, u32[]{:S(2)}, u32[]{:S(2)}) %all-to-all-start.2) | async-done | bytes 196640 | tf_op jit(solution)/shard_map/all_to_all | solution.py:182
  173.6 1.8 copy.66
  179.0 1.9 reshape.475
  182.0 1.9 multiply_convert_fusion
  185.2 2.0 fusion.7
  188.8 2.8 fusion.6
  193.3 2.3 fusion.5
  199.1 7.3 %collective-permute-done = bf16[1,1,128,3,1,192]{2,5,0,3,4,1:T(8,128)(2,1)S(1)} collective-permute-done((bf16[1,1,128,3,1,192]{2,5,0,3,4,1:T(8,128)(2,1)S(1)}, bf16[1,1,128,3,1,192]{2,5,0,3,4,1:T(8,128)(2,1)S(1)}, u32[]{:S(2)}, u32[]{:S(2)}) %collective-permute-start) | collective-permute-done | bytes 147488 | tf_op jit(solution)/shard_map/ppermute | solution.py:231
  206.9 6.7 %collective-permute-done.1 = bf16[1,1,128,3,1,192]{2,5,0,3,4,1:T(8,128)(2,1)S(1)} collective-permute-done((bf16[1,1,128,3,1,192]{2,5,0,3,4,1:T(8,128)(2,1)S(1)}, bf16[1,1,128,3,1,192]{2,5,0,3,4,1:T(8,128)(2,1)S(1)}, u32[]{:S(2)}, u32[]{:S(2)}) %collective-permute-start.1) | collective-permute-done | bytes 147488 | tf_op jit(solution)/shard_map/ppermute | solution.py:231
  214.6 4.1 fusion.49
  218.8 1.8 convert_element_type.247
  220.7 19.0 %reduce-scatter.23.cloned.1.call-done = f32[1152,96]{0,1:T(8,128)} async-done(((f32[1152,768]{0,1:T(8,128)}), f32[1152,96]{0,1:T(8,128)}) %reduce-scatter.23.cloned.1.call-update) | async-done | bytes 442384 | tf_op jit(solution)/shard_map/reduce_scatter | solution.py:260
  241.4 67.2 %reduce-scatter.19.cloned.1.call-done = f32[96,2304]{1,0:T(8,128)} async-done(((f32[768,2304]{1,0:T(8,128)}), f32[96,2304]{1,0:T(8,128)}) %reduce-scatter.19.cloned.1.call-update) | async-done | bytes 884752 | tf_op jit(solution)/shard_map/reduce_scatter | solution.py:259
  308.7 2.0 convert_element_type.249
  314.0 3.5 fusion.34
  317.4 60.3 %reduce-scatter.11.cloned.1.call-done = f32[96,2304]{1,0:T(8,128)} async-done(((f32[768,2304]{1,0:T(8,128)}), f32[96,2304]{1,0:T(8,128)}) %reduce-scatter.11.cloned.1.call-update) | async-done | bytes 884752 | tf_op jit(solution)/shard_map/reduce_scatter | solution.py:257
  377.7 2.0 convert_element_type.245
  379.8 12.8 %all-reduce.9 = (bf16[768]{0:T(1024)(128)(2,1)S(1)}, bf16[768]{0:T(1024)(128)(2,1)S(1)}) all-reduce(f32[768]{0:T(1024)S(1)} %get-tuple-element.48, f32[768]{0:T(1024)S(1)} %copy-done.24), channel_id=10, replica_groups=mesh['seq'=4,'fsdp'=8] {'fsdp'}, use_global_device_ids=true, to_apply=%region_20.21.clone | all-reduce | flops 1536 | bytes 9216
  392.7 11.7 %all-reduce.12 = (bf16[96]{0:T(256)(128)(2,1)S(1)}, bf16[96]{0:T(256)(128)(2,1)S(1)}) all-reduce(bf16[96]{0:T(256)(128)(2,1)S(1)} %dynamic-slice.19, bf16[96]{0:T(256)(128)(2,1)S(1)} %dynamic-slice.18), channel_id=11, replica_groups=mesh['seq'=4,'fsdp'=8] {'seq'}, use_global_device_ids=true, to_apply=%region_21.22.clone | all-reduce | flops 192 | bytes 768
  404.9 8.3 %all-reduce.11 = (bf16[96]{0:T(256)(128)(2,1)S(1)}, bf16[96]{0:T(256)(128)(2,1)S(1)}) all-reduce(bf16[96]{0:T(256)(128)(2,1)S(1)} %dynamic-update-slice.2, bf16[96]{0:T(256)(128)(2,1)S(1)} %dynamic-update-slice.3), channel_id=1, replica_groups=mesh['seq'=4,'fsdp'=8] {'seq'}, use_global_device_ids=true, to_apply=%add.2 | all-reduce | flops 192 | bytes 768
  415.2 13.9 %all_gather.49 = bf16[96,768]{1,0:T(8,128)(2,1)S(1)} all-gather(bf16[24,768]{1,0:T(8,128)(2,1)} %reduce-scatter.17.cloned.1.call-done), channel_id=1, replica_groups=mesh['seq'=4,'fsdp'=8] {'seq'}, dimensions={0}, use_global_device_ids=true | all-gather | bytes 184320 | tf_op jit(solution)/shard_map/all_gather | solution.py:288
  429.8 14.9 %all_gather.51 = bf16[1152,96]{0,1:T(8,128)(2,1)S(1)} all-gather(bf16[1152,24]{0,1:T(8,128)(2,1)} %reduce-scatter.25.cloned.1.call-done), channel_id=1, replica_groups=mesh['seq'=4,'fsdp'=8] {'seq'}, dimensions={1}, use_global_device_ids=true | all-gather | bytes 276480 | tf_op jit(solution)/shard_map/all_gather | solution.py:294
  445.5 17.3 %all_gather.50 = bf16[96,2304]{1,0:T(8,128)(2,1)S(1)} all-gather(bf16[24,2304]{1,0:T(8,128)(2,1)} %reduce-scatter.21.cloned.1.call-done), channel_id=1, replica_groups=mesh['seq'=4,'fsdp'=8] {'seq'}, dimensions={0}, use_global_device_ids=true | all-gather | bytes 552960 | tf_op jit(solution)/shard_map/all_gather | solution.py:291
  463.8 2.6 reduce-scatter.13.cloned.1.call-done
  466.4 15.6 %all_gather.48 = bf16[96,2304]{1,0:T(8,128)(2,1)S(1)} all-gather(bf16[24,2304]{1,0:T(8,128)(2,1)} %reduce-scatter.13.cloned.1.call-done), channel_id=1, replica_groups=mesh['seq'=4,'fsdp'=8] {'seq'}, dimensions={0}, use_global_device_ids=true | all-gather | bytes 552960 | tf_op jit(solution)/shard_map/all_gather | solution.py:285
  (162 shorter events, 49.0 us)
Async XLA Ops:
  7.2 39.4 %all-gather.5.cloned.1.call-start = ((), (), s32[]{:S(2)}) async-start(), calls=%async_computation.11 | async-start | bytes 3981312 | tf_op jit(solution)/shard_map/all_gather | solution.py:105
  7.9 95.4 %all-gather.7.cloned.1.call-start = ((), (), s32[]{:S(2)}) async-start(), calls=%async_computation.12 | async-start | bytes 1327104 | tf_op jit(solution)/shard_map/all_gather | solution.py:106
  8.6 99.5 %all-gather.9.cloned.1.call-start = ((), (), s32[]{:S(2)}) async-start(), calls=%async_computation.13 | async-start | bytes 3981312 | tf_op jit(solution)/shard_map/all_gather | solution.py:107
  30.2 20.8 %copy-start.17 = (f32[128]{0:T(128)}, f32[128]{0:T(128)S(1)}, u32[]{:S(2)}) copy-start(f32[128]{0:T(128)S(1)} %broadcast_multiply_fusion.5) | copy-start | bytes 1540
  31.4 19.7 %copy-start.21 = (f32[128]{0:T(128)}, f32[128]{0:T(128)S(1)}, u32[]{:S(2)}) copy-start(f32[128]{0:T(128)S(1)} %add_rsqrt_fusion.1) | copy-start | bytes 1540
  51.1 2.2 copy-start.13
  51.1 2.2 copy-start.15
  54.4 20.9 %all-to-all-start = ((bf16[1,128,3,4,192]{1,4,2,0,3:T(8,128)(2,1)}), bf16[1,128,3,4,192]{1,4,2,0,3:T(8,128)(2,1)S(1)}, u32[]{:S(2)}, u32[]{:S(2)}) async-start(bf16[1,128,3,4,192]{1,4,2,0,3:T(8,128)(2,1)} %pad_maximum_fusion), calls=%async_computation | async-start | bytes 1179648 | tf_op jit(solution)/shard_map/all_to_all | solution.py:126
  59.0 77.3 %all-gather.11.cloned.1.call-start = ((), (), s32[]{:S(2)}) async-start(), calls=%async_computation.14 | async-start | bytes 1990656 | tf_op jit(solution)/shard_map/all_gather | solution.py:108
  80.6 22.7 %copy-start.8 = (bf16[3,64,512]{2,1,0:T(8,128)(2,1)}, bf16[3,64,512]{2,1,0:T(8,128)(2,1)S(1)}, u32[]{:S(2)}) copy-start(bf16[3,64,512]{2,1,0:T(8,128)(2,1)S(1)} %convolution_convert_fusion.2) | copy-start | bytes 589828
  88.1 10.6 %all-to-all-start.1 = ((bf16[4,2,12288]{2,1,0:T(2,128)(2,1)}), bf16[4,2,12288]{2,1,0:T(2,128)(2,1)S(1)}, u32[]{:S(2)}, u32[]{:S(2)}) async-start(bf16[4,2,12288]{2,1,0:T(2,128)(2,1)} %reshape.503), calls=%async_computation.1 | async-start | bytes 393216 | tf_op jit(solution)/shard_map/all_to_all | solution.py:148
  91.4 127.4 %reduce-scatter.15.cloned.1.call-start = ((), (), s32[]{:S(2)}) async-start(), calls=%async_computation.17 | async-start | bytes 2654208 | tf_op jit(solution)/shard_map/reduce_scatter | solution.py:258
  105.1 0.5 copy-start.19
  136.3 4.6 copy-start.4
  136.3 4.6 copy-start.20
  136.3 4.6 copy-start.23
  140.9 2.2 copy-start.11
  140.9 2.2 copy-start.12
  140.9 2.0 copy-start.10
  141.0 2.9 copy-start.7
  143.1 0.7 copy-start.2
  145.8 93.8 %reduce-scatter.23.cloned.1.call-start = ((), (), s32[]{:S(2)}) async-start(), calls=%async_computation.21 | async-start | bytes 3981312 | tf_op jit(solution)/shard_map/reduce_scatter | solution.py:260
  147.2 0.7 copy-start.5
  151.2 157.4 %reduce-scatter.19.cloned.1.call-start = ((), (), s32[]{:S(2)}) async-start(), calls=%async_computation.19 | async-start | bytes 7962624 | tf_op jit(solution)/shard_map/reduce_scatter | solution.py:259
  161.0 12.6 %all-to-all-start.2 = ((bf16[1,128,4,192]{1,3,0,2:T(8,128)(2,1)}), bf16[1,128,4,192]{1,3,0,2:T(8,128)(2,1)}, u32[]{:S(2)}, u32[]{:S(2)}) async-start(bf16[1,128,4,192]{1,3,0,2:T(8,128)(2,1)} %bitcast.196), calls=%async_computation.2 | async-start | bytes 393216 | tf_op jit(solution)/shard_map/all_to_all | solution.py:182
  165.6 212.2 %reduce-scatter.11.cloned.1.call-start = ((), (), s32[]{:S(2)}) async-start(), calls=%async_computation.15 | async-start | bytes 7962624 | tf_op jit(solution)/shard_map/reduce_scatter | solution.py:257
  183.9 1.2 copy-start
  197.5 16.4 %copy-start.14 = (f32[128,32]{0,1:T(8,128)S(1)}, f32[128,32]{0,1:T(8,128)}, u32[]{:S(2)}) copy-start(f32[128,32]{0,1:T(8,128)} %get-tuple-element.92) | copy-start | bytes 49156
  197.5 16.4 %copy-start.16 = (f32[128,32]{0,1:T(8,128)S(1)}, f32[128,32]{0,1:T(8,128)}, u32[]{:S(2)}) copy-start(f32[128,32]{0,1:T(8,128)} %get-tuple-element.93) | copy-start | bytes 49156
  198.6 7.8 %collective-permute-start = (bf16[1,1,128,3,1,192]{2,5,0,3,4,1:T(8,128)(2,1)S(1)}, bf16[1,1,128,3,1,192]{2,5,0,3,4,1:T(8,128)(2,1)S(1)}, u32[]{:S(2)}, u32[]{:S(2)}) collective-permute-start(bf16[1,1,128,3,1,192]{2,5,0,3,4,1:T(8,128)(2,1)S(1)} %constant_dynamic-slice_fusion.2), channel_id=1, source_target_pairs={{0,8},{8,16},{16,24},{24,0},{1,9},{9,17},{17,25},{25,1},{2,10},{10... | collective-permute-start | bytes 442376 | tf_op jit(solution)/shard_map/ppermute | solution.py:231
  206.5 7.1 %collective-permute-start.1 = (bf16[1,1,128,3,1,192]{2,5,0,3,4,1:T(8,128)(2,1)S(1)}, bf16[1,1,128,3,1,192]{2,5,0,3,4,1:T(8,128)(2,1)S(1)}, u32[]{:S(2)}, u32[]{:S(2)}) collective-permute-start(bf16[1,1,128,3,1,192]{2,5,0,3,4,1:T(8,128)(2,1)S(1)} %get-tuple-element.78), channel_id=1, source_target_pairs={{0,16},{8,24},{16,0},{24,8},{1,17},{9,25},{17,1},{25,9},{2,18},{10... | collective-permute-start | bytes 442376 | tf_op jit(solution)/shard_map/ppermute | solution.py:231
  206.5 7.0 %collective-permute-start.2 = (bf16[1,1,128,3,1,192]{2,5,0,3,4,1:T(8,128)(2,1)S(1)}, bf16[1,1,128,3,1,192]{2,5,0,3,4,1:T(8,128)(2,1)S(1)}, u32[]{:S(2)}, u32[]{:S(2)}) collective-permute-start(bf16[1,1,128,3,1,192]{2,5,0,3,4,1:T(8,128)(2,1)S(1)} %get-tuple-element.77), channel_id=1, source_target_pairs={{0,24},{8,0},{16,8},{24,16},{1,25},{9,1},{17,9},{25,17},{2,26},{10... | collective-permute-start | bytes 442376 | tf_op jit(solution)/shard_map/ppermute | solution.py:231
  213.6 0.9 copy-start.1
  213.6 0.9 copy-start.18
  213.6 0.9 copy-start.22
  218.7 93.9 %copy-start.6 = (bf16[128,1152]{1,0:T(8,128)(2,1)S(1)}, bf16[128,1152]{1,0:T(8,128)(2,1)}, u32[]{:S(2)}) copy-start(bf16[128,1152]{1,0:T(8,128)(2,1)} %copy-done.5) | copy-start | bytes 884740
  218.7 93.9 %copy-start.9 = (bf16[1152,768]{0,1:T(8,128)(2,1)S(1)}, bf16[1152,768]{0,1:T(8,128)(2,1)}, u32[]{:S(2)}) copy-start(bf16[1152,768]{0,1:T(8,128)(2,1)} %all-gather.11.cloned.1.call-done) | copy-start | bytes 5308420
  218.7 196.4 %reduce-scatter.17.cloned.1.call-start = ((), (), s32[]{:S(2)}) async-start(), calls=%async_computation.18 | async-start | bytes 184320 | tf_op jit(solution)/shard_map/reduce_scatter | solution.py:268
  220.6 209.2 %reduce-scatter.25.cloned.1.call-start = ((), (), s32[]{:S(2)}) async-start(), calls=%async_computation.22 | async-start | bytes 276480
  241.4 204.1 %reduce-scatter.21.cloned.1.call-start = ((), (), s32[]{:S(2)}) async-start(), calls=%async_computation.20 | async-start | bytes 552960 | tf_op jit(solution)/shard_map/reduce_scatter | solution.py:271
  310.7 155.7 %reduce-scatter.13.cloned.1.call-start = ((), (), s32[]{:S(2)}) async-start(), calls=%async_computation.16 | async-start | bytes 552960 | tf_op jit(solution)/shard_map/reduce_scatter | solution.py:265
  314.0 65.8 %copy-start.24 = (f32[768]{0:T(1024)S(1)}, f32[768]{0:T(1024)}, u32[]{:S(2)}) copy-start(f32[768]{0:T(1024)} %get-tuple-element.46) | copy-start | bytes 9220
  314.0 100.3 %copy-start.3 = (f32[128,768]{1,0:T(8,128)S(1)}, f32[128,768]{1,0:T(8,128)}, u32[]{:S(2)}) copy-start(f32[128,768]{1,0:T(8,128)} %copy-done.2) | copy-start | bytes 1179652
Sparse Core Ops, SparseCore 0:
  9.9 36.6 all-gather.4
  48.4 23.9 all-gather.6
  74.3 33.8 all-gather.8
  109.9 26.3 all-gather.10
  145.9 42.3 reduce-scatter.14
  191.6 47.9 reduce-scatter.22
  243.1 65.4 reduce-scatter.18
  312.2 65.4 reduce-scatter.10
  380.0 19.5 reduce-scatter.16
  401.7 17.8 reduce-scatter.24
  422.4 21.0 reduce-scatter.20
  446.3 20.0 reduce-scatter.12
